TPU v7x, 512 devices: a whole 4x8x8 slice. The times are simulated.
512 devices in a mesh: dom: 16 (over z_hi, y), rel: 32 (over z_lo, x, core).
Axes of the slice: x: 4, y: 8, z: 8 (z_hi: 2, z_lo: 4; z = z_hi * 4 + z_lo), core: 2. Of those that a mesh axis runs over, the one named last changes fastest.
Arguments:
- entity: float32 [65536, 512], P(('dom', 'rel')), may hold values from -1.8 to 1.8
- entity_acc: float32 [65536, 512], P(('dom', 'rel')), may hold values from 0.01 to 1
- relation: float32 [4096, 512], P('rel'), may hold values from -1 to 1, as said below
- relation_acc: float32 [4096, 512], P('rel'), may hold values from 0.01 to 1
- send_rows: int32 [512, 32, 16], P(('dom', 'rel')), may hold values from 0 to 127, as said below
- trip_head: int32 [131072], P(('dom', 'rel')), may hold values from 0 to 511
- trip_rel: int32 [131072], P(('dom', 'rel')), may hold values from 0 to 127
- trip_tail: int32 [131072], P(('dom', 'rel')), may hold values from 0 to 511
- neg_part: int32 [1], replicated, may hold values from 0 to 15
- neg_rows: int32 [32, 32], replicated, may hold values from 0 to 127
Outputs:
- new_entity: float32 [65536, 512], P(('dom', 'rel'))
- new_entity_acc: float32 [65536, 512], P(('dom', 'rel'))
- new_relation: float32 [4096, 512], P('rel')
- new_relation_acc: float32 [4096, 512], P('rel')
Inputs may be any that keep to these rules, and one draw needn't show every extreme that they name: `send_rows`: within one owner's list for one receiver the 16 rows are distinct. `relation`: every component has magnitude 0.1 or more.
All inputs are finite; a program needn't handle non-finite values.
Results may differ from a plain program's by a relative error of at most 0.0003.
Values sent between devices are 32-bit elements; how exact they have to be, the bound alone decides.
A program may use at most 64 MiB of HBM per device.

v0:
```python
import jax
import jax.numpy as jnp
from jax import lax
from jax.sharding import PartitionSpec as P

step_size = 0.05


def broadcast(block, axis, owner):
    block = jnp.where(lax.axis_index(axis) == owner, block, jnp.zeros_like(block))
    return lax.psum(block, axis)


def hamilton(left, right):
    left_a, left_b, left_c, left_d = jnp.split(left, 4, axis=-1)
    right_a, right_b, right_c, right_d = jnp.split(right, 4, axis=-1)
    out_a = left_a * right_a - left_b * right_b - left_c * right_c - left_d * right_d
    out_b = left_a * right_b + left_b * right_a + left_c * right_d - left_d * right_c
    out_c = left_a * right_c - left_b * right_d + left_c * right_a + left_d * right_b
    out_d = left_a * right_d + left_b * right_c - left_c * right_b + left_d * right_a
    return jnp.concatenate([out_a, out_b, out_c, out_d], axis=-1)


def unit_rel(relation):
    comp_a, comp_b, comp_c, comp_d = jnp.split(relation, 4, axis=-1)
    magnitude = jnp.sqrt(comp_a * comp_a + comp_b * comp_b + comp_c * comp_c + comp_d * comp_d)
    return relation / jnp.concatenate([magnitude, magnitude, magnitude, magnitude], axis=-1)


def local_loss(touched, relation, negatives, heads, rels, tails):
    unit_rows = unit_rel(relation)
    one_hot = (rels[:, None] == jnp.arange(relation.shape[0])[None, :]).astype(unit_rows.dtype)
    rotation = jnp.dot(one_hot, unit_rows, precision=lax.Precision.HIGHEST)
    query = hamilton(touched[heads], rotation)
    positive = jnp.sum(query * touched[tails], axis=-1)
    scores = jnp.einsum("ik,jk->ij", query, negatives, precision=lax.Precision.HIGHEST)
    return (
        jnp.sum(jax.nn.softplus(-positive)) + jnp.sum(jax.nn.softplus(scores)) / negatives.shape[0]
    )


def adagrad(values, history, gradient):
    history_new = history + gradient * gradient
    return (values - step_size * gradient / jnp.sqrt(history_new), history_new)


def shards(
    entity,
    entity_acc,
    relation,
    relation_acc,
    send_rows,
    trip_head,
    trip_rel,
    trip_tail,
    neg_part,
    neg_rows,
):
    row_width = entity.shape[1]
    send_lists = send_rows[0]
    outgoing = entity[send_lists]
    touched = lax.all_to_all(outgoing, "rel", split_axis=0, concat_axis=0, tiled=True).reshape(
        -1, row_width
    )
    neg_root = neg_part[0]
    rel_here = lax.axis_index("rel")
    own_negs = entity[neg_rows[rel_here]]
    grouped = lax.all_gather(own_negs, "rel", axis=0, tiled=True)
    negatives = broadcast(grouped, "dom", neg_root)

    def scored(touched_in, relation_in, negatives_in):
        return local_loss(touched_in, relation_in, negatives_in, trip_head, trip_rel, trip_tail)

    loss_value, pullback = jax.vjp(scored, touched, relation, negatives)
    grad_rows, grad_rel, grad_neg = pullback(jnp.ones_like(loss_value))
    returned = lax.all_to_all(
        grad_rows.reshape(-1, send_lists.shape[1], row_width),
        "rel",
        split_axis=0,
        concat_axis=0,
        tiled=True,
    )
    ent_grad = jnp.zeros_like(entity).at[send_lists].add(returned)
    neg_share = lax.psum_scatter(grad_neg, "rel", scatter_dimension=0, tiled=True)
    neg_total = lax.psum(neg_share, "dom")
    is_owner = (lax.axis_index("dom") == neg_root).astype(jnp.float32)
    ent_grad = ent_grad.at[neg_rows[rel_here]].add(is_owner * neg_total)
    new_entity, new_entity_acc = adagrad(entity, entity_acc, ent_grad)
    rel_sum = lax.psum(grad_rel, "dom")
    new_relation, new_relation_acc = adagrad(relation, relation_acc, rel_sum)
    return (new_entity, new_entity_acc, new_relation, new_relation_acc)


def solution(mesh):
    in_specs = (
        P(("dom", "rel"), None),
        P(("dom", "rel"), None),
        P("rel", None),
        P("rel", None),
        P(("dom", "rel"), None, None),
        P(("dom", "rel")),
        P(("dom", "rel")),
        P(("dom", "rel")),
        P(),
        P(),
    )
    out_specs = (P(("dom", "rel"), None), P(("dom", "rel"), None), P("rel", None), P("rel", None))
    return jax.shard_map(shards, mesh=mesh, in_specs=in_specs, out_specs=out_specs, check_vma=False)
```

profile of v0, /device:TPU:8, one launch (start us, length us, event | category | flops | bytes accessed | tf_op | source)
XLA Modules:
  0.0 652.1 jit_solution(494855978399194900)
XLA Ops:
  7.2 0.0 copy-start
  7.2 0.0 all-gather.3.cloned.1.call-start
  7.2 0.7 fusion.40
  8.0 2.2 gather_fusion.3
  10.2 0.0 all-gather.3.cloned.1.call-update
  10.2 0.7 compare_select_fusion.3
  10.9 0.1 copy.14
  11.0 0.1 reshape.123
  11.1 0.0 copy-done
  11.1 2.3 gather_fusion
  13.4 10.1 %all-to-all-start = ((f32[32,16,512]{2,1,0:T(8,128)}), f32[32,16,512]{2,1,0:T(8,128)S(1)}, u32[]{:S(2)}, u32[]{:S(2)}) async-start(f32[32,16,512]{2,1,0:T(8,128)} %bitcast.1), calls=%async_computation | async-start | bytes 2097152 | tf_op jit(solution)/shard_map/all_to_all | solution.py:62
  23.5 0.0 all-reduce.4.cloned.1.call-start
  24.2 57.4 %all-gather.3.cloned.1.call-done = f32[1024,512]{1,0:T(8,128)} async-done(((f32[32,512]{1,0:T(8,128)}), f32[1024,512]{1,0:T(8,128)}) %all-gather.3.cloned.1.call-update) | async-done | bytes 2097168 | tf_op jit(solution)/shard_map/all_gather | solution.py:68
  81.6 1.6 broadcast_select_fusion
  83.2 0.0 all-reduce.4.cloned.1.call-update
  83.2 0.0 reduce-scatter.2.cloned.1.call-start
  83.3 0.6 copy-done.12
  83.9 0.3 copy-done.1
  84.2 0.0 copy-done.14
  84.2 0.0 copy-start.10
  84.2 0.4 fusion.24
  84.7 0.0 all-to-all-done
  84.7 0.2 copy-done.10
  84.8 1.0 gather_fusion.1
  85.8 0.1 multiply_add_fusion.11
  85.9 0.0 copy-start.4
  85.9 0.1 multiply_subtract_fusion.3
  86.0 0.0 copy-start.5
  86.0 0.0 copy-start.6
  86.0 205.6 %all-reduce.4.cloned.1.call-done = f32[1024,512]{1,0:T(8,128)} async-done(((f32[1024,512]{1,0:T(8,128)}), f32[1024,512]{1,0:T(8,128)}) %all-reduce.4.cloned.1.call-update) | async-done | bytes 2097168 | tf_op jit(solution)/shard_map/psum | solution.py:11
  291.6 3.5 fusion.49
  295.1 0.0 copy-start.7
  295.1 1.0 copy-done.7
  296.1 3.9 fusion.28
  300.0 0.0 reduce-scatter.2.cloned.1.call-update
  300.0 0.7 copy-done.13
  300.7 1.0 gather_fusion.2
  301.7 0.0 copy-done.4
  301.7 0.0 copy-done.5
  301.7 0.0 copy-done.6
  301.7 0.1 multiply_reduce_fusion
  301.8 0.7 copy-done.3
  302.5 3.1 scatter_custom_fusion
  305.6 4.7 convolution_add_fusion
  310.4 0.1 multiply_add_fusion.9
  310.4 0.1 multiply_add_fusion.7
  310.5 3.1 scatter_custom_fusion.1
  313.7 2.4 add_any.115
  316.1 5.3 all-to-all-start.1
  321.4 0.0 all-reduce.6.cloned.1.call-start
  321.5 0.1 multiply_add_fusion.4
  321.6 0.1 multiply_add_fusion.5
  321.7 0.0 copy-start.8
  321.7 0.0 copy-start.9
  321.7 0.4 multiply_negate_fusion
  322.1 0.1 add_multiply_fusion.3
  322.2 0.7 maximum_add_fusion
  322.9 127.9 %reduce-scatter.2.cloned.1.call-done = f32[32,512]{1,0:T(8,128)} async-done(((f32[1024,512]{1,0:T(8,128)}), f32[32,512]{1,0:T(8,128)}) %reduce-scatter.2.cloned.1.call-update) | async-done | bytes 65552 | tf_op jit(solution)/shard_map/reduce_scatter | solution.py:84
  450.8 0.0 all-reduce.6.cloned.1.call-update
  450.9 0.0 all-to-all-done.1
  450.9 3.6 scatter_custom_fusion.2
  454.5 187.9 %all-reduce.6.cloned.1.call-done = (f32[32,512]{1,0:T(8,128)}, f32[128,512]{1,0:T(8,128)}) async-done(((f32[32,512]{1,0:T(8,128)}, f32[128,512]{1,0:T(8,128)}), (f32[32,512]{1,0:T(8,128)}, f32[128,512]{1,0:T(8,128)})) %all-reduce.6.cloned.1.call-update) | async-done | bytes 327696 | tf_op jit(solution)/shard_map/psum | solution.py:85
  642.4 1.2 scatter_custom_fusion.3
  643.6 2.0 multiply_subtract_fusion
  (22 shorter events, 0.1 us)
Async XLA Ops:
  7.2 3.9 copy-start
  7.2 74.5 %all-gather.3.cloned.1.call-start = ((), (), s32[]{:S(2)}) async-start(), calls=%async_computation.5 | async-start | bytes 2162688 | tf_op jit(solution)/shard_map/all_gather | solution.py:68
  13.4 71.3 %all-to-all-start = ((f32[32,16,512]{2,1,0:T(8,128)}), f32[32,16,512]{2,1,0:T(8,128)S(1)}, u32[]{:S(2)}, u32[]{:S(2)}) async-start(f32[32,16,512]{2,1,0:T(8,128)} %bitcast.1), calls=%async_computation | async-start | bytes 2097152 | tf_op jit(solution)/shard_map/all_to_all | solution.py:62
  23.5 268.0 %all-reduce.4.cloned.1.call-start = ((), (), s32[]{:S(2)}) async-start(), calls=%async_computation.3 | async-start | bytes 4194304 | tf_op jit(solution)/shard_map/psum | solution.py:11
  83.2 0.7 copy-start.12
  83.2 1.0 copy-start.1
  83.2 1.0 copy-start.14
  83.2 367.6 %reduce-scatter.2.cloned.1.call-start = ((), (), s32[]{:S(2)}) async-start(), calls=%async_computation.4 | async-start | bytes 2162688 | tf_op jit(solution)/shard_map/reduce_scatter | solution.py:84
  84.2 0.6 copy-start.10
  85.9 215.8 %copy-start.4 = (f32[256,128]{1,0:T(8,128)}, f32[256,128]{1,0:T(8,128)S(1)}, u32[]{:S(2)}) copy-start(f32[256,128]{1,0:T(8,128)S(1)} %get-tuple-element.23) | copy-start | bytes 393220
  86.0 215.7 %copy-start.5 = (f32[256,128]{1,0:T(8,128)}, f32[256,128]{1,0:T(8,128)S(1)}, u32[]{:S(2)}) copy-start(f32[256,128]{1,0:T(8,128)S(1)} %get-tuple-element.20) | copy-start | bytes 393220
  86.0 215.7 %copy-start.6 = (f32[256,128]{1,0:T(8,128)}, f32[256,128]{1,0:T(8,128)S(1)}, u32[]{:S(2)}) copy-start(f32[256,128]{1,0:T(8,128)S(1)} %get-tuple-element.21) | copy-start | bytes 393220
  295.1 1.0 copy-start.7
  300.0 0.7 copy-start.13
  301.7 0.8 copy-start.3
  316.1 5.6 copy-start.2
  316.1 5.6 copy-start.11
  316.1 5.6 copy-start.15
  316.1 134.8 %all-to-all-start.1 = ((f32[32,16,512]{2,1,0:T(8,128)}), f32[32,16,512]{2,1,0:T(8,128)S(1)}, u32[]{:S(2)}, u32[]{:S(2)}) async-start(f32[32,16,512]{2,1,0:T(8,128)} %bitcast.6), calls=%async_computation.1 | async-start | bytes 2097152 | tf_op jit(solution)/shard_map/all_to_all | solution.py:76
  321.4 321.0 %all-reduce.6.cloned.1.call-start = ((), (), s32[]{:S(2)}) async-start(), calls=%async_computation.6 | async-start | bytes 655360 | tf_op jit(solution)/shard_map/psum | solution.py:85
  321.7 321.9 %copy-start.8 = (f32[128,512]{1,0:T(8,128)S(1)}, f32[128,512]{1,0:T(8,128)}, u32[]{:S(2)}) copy-start(f32[128,512]{1,0:T(8,128)} %param.13) | copy-start | bytes 786436
  321.7 321.9 %copy-start.9 = (f32[128,512]{1,0:T(8,128)S(1)}, f32[128,512]{1,0:T(8,128)}, u32[]{:S(2)}) copy-start(f32[128,512]{1,0:T(8,128)} %param.11) | copy-start | bytes 786436
Sparse Core Ops, SparseCore 0:
  10.7 70.8 all-gather.2
  84.6 206.9 all-reduce.3
  300.1 150.6 reduce-scatter.1
  454.3 188.0 all-reduce.5
where the time goes:
time: 653 us; the launch traced here: 652 us
  waiting for transfers between devices  579 us (89%)
  other arithmetic  20 us (3%)
  starting transfers between devices  15.6 us (2%)
  between operations  14.7 us (2%)
  matrix products  13 us (2%)
  local copies, waits for them, and re-layouts  10.1 us (2%)
    psum x1, waiting for transfers between devices, broadcast(): return lax.psum(block, axis)  206 us
    psum x1, waiting for transfers between devices, shards(): neg_total = lax.psum(neg_share, 'dom')  188 us
    reduce_scatter x1, waiting for transfers between devices, shards(): lax.psum_scatter(grad_neg, 'rel', scatter_dimension=0, tiled=True)  128 us
    all_gather x1, waiting for transfers between devices, shards(): grouped = lax.all_gather(own_negs, 'rel', axis=0, tiled=True)  57.4 us
  transfers between devices with their start and end apart: 6, of which 4 were waited for; matrix products, arithmetic and copies ran while one was open for 4% of the time, Pallas kernels for 0%

commit v1 on v0

--- a/solution.py
+++ b/solution.py
@@ -6,9 +6,15 @@
 step_size = 0.05
 
 
+def add_all(x, mesh_axis):
+    parts = lax.all_gather(x, mesh_axis, axis=0, tiled=False)
+    total = parts.sum(axis=0)
+    return total
+
+
 def broadcast(block, axis, owner):
     block = jnp.where(lax.axis_index(axis) == owner, block, jnp.zeros_like(block))
-    return lax.psum(block, axis)
+    return add_all(block, axis)
 
 
 def hamilton(left, right):

time: 653 us -> 1090 us (1.67)
  waiting for transfers between devices: 579 us -> 1010 us
  other arithmetic: 20 us -> 33.2 us
    all_gather x0 -> x1, waiting for transfers between devices: none -> 555 us  [add_all(): parts = lax.all_gather(x, mesh_axis, axis=0, tiled=False)]
    psum x1 -> x0, waiting for transfers between devices: 206 us -> none  [broadcast(): return lax.psum(block, axis)]
    all_to_all x1, waiting for transfers between devices: 0.01 us -> 70.6 us  [shards(): lax.all_to_all(outgoing, 'rel', split_axis=0, concat_axis=0, tiled=True)]
    reduce_sum x0 -> x1, other arithmetic: none -> 14 us  [add_all(): total = parts.sum(axis=0)]
  transfers between devices with their start and end apart: 6 -> 6, of which waited for: 4 -> 5; matrix products, arithmetic and copies ran while one was open for 4% -> 2% of each run, Pallas kernels for 0% -> 0%
where the time goes in v1:
time: 1090 us
  waiting for transfers between devices  1010 us (93%)
  other arithmetic  33.2 us (3%)
  between operations  14.8 us (1%)
  matrix products  12.3 us (1%)
  local copies, waits for them, and re-layouts  11 us (1%)
    all_gather x1, waiting for transfers between devices, add_all(): parts = lax.all_gather(x, mesh_axis, axis=0, tiled=False)  555 us
    psum x1, waiting for transfers between devices, shards(): neg_total = lax.psum(neg_share, 'dom')  188 us
    reduce_scatter x1, waiting for transfers between devices, shards(): lax.psum_scatter(grad_neg, 'rel', scatter_dimension=0, tiled=True)  126 us
    all_to_all x1, waiting for transfers between devices, shards(): lax.all_to_all(outgoing, 'rel', split_axis=0, concat_axis=0, tiled=True)  70.6 us
    all_gather x1, waiting for transfers between devices, shards(): grouped = lax.all_gather(own_negs, 'rel', axis=0, tiled=True)  66.8 us
  transfers between devices with their start and end apart: 6, of which 5 were waited for; matrix products, arithmetic and copies ran while one was open for 2% of the time, Pallas kernels for 0%

profile of v1, /device:TPU:8, one launch (start us, length us, event | category | flops | bytes accessed | tf_op | source)
XLA Modules:
  0.0 1088.0 jit_solution(16946602358131385647)
XLA Ops:
  7.2 0.0 all-gather.5.cloned.1.call-start
  7.2 0.7 fusion.40
  7.9 0.5 copy-done.18
  8.5 2.2 gather_fusion.3
  10.7 0.0 all-gather.5.cloned.1.call-update
  10.7 0.0 all-gather.7.cloned.1.call-start
  11.4 66.8 %all-gather.5.cloned.1.call-done = f32[1024,512]{1,0:T(8,128)} async-done(((f32[32,512]{1,0:T(8,128)}), f32[1024,512]{1,0:T(8,128)}) %all-gather.5.cloned.1.call-update) | async-done | bytes 2097168 | tf_op jit(solution)/shard_map/all_gather | solution.py:74
  78.2 1.5 broadcast_select_fusion
  79.7 0.0 all-gather.7.cloned.1.call-update
  79.7 0.7 copy-done.15
  80.4 0.1 copy.14
  80.5 0.1 reshape.123
  80.6 0.1 copy-done
  80.7 2.3 gather_fusion
  83.0 5.4 all-to-all-start
  88.4 0.0 reduce-scatter.2.cloned.1.call-start
  88.5 0.0 copy-done.16
  88.6 0.0 copy-start.13
  88.6 0.4 fusion.24
  89.0 70.6 %all-to-all-done = f32[32,16,512]{2,1,0:T(8,128)S(1)} async-done(((f32[32,16,512]{2,1,0:T(8,128)}), f32[32,16,512]{2,1,0:T(8,128)S(1)}, u32[]{:S(2)}, u32[]{:S(2)}) %all-to-all-start) | async-done | bytes 1048608 | tf_op jit(solution)/shard_map/all_to_all | solution.py:68
  159.6 1.0 gather_fusion.1
  160.6 0.1 multiply_add_fusion.11
  160.6 0.0 copy-start.7
  160.7 0.1 multiply_subtract_fusion.3
  160.7 0.0 copy-start.8
  160.7 0.0 copy-start.9
  160.8 555.0 %all-gather.7.cloned.1.call-done = f32[16384,512]{1,0:T(8,128)} async-done(((f32[1024,512]{1,0:T(8,128)}), f32[16384,512]{1,0:T(8,128)}) %all-gather.7.cloned.1.call-update) | async-done | bytes 33554448 | tf_op jit(solution)/shard_map/all_gather | solution.py:10
  715.7 14.0 %reduce_sum.19 = f32[1024,512]{1,0:T(8,128)} reduce(f32[16,1024,512]{2,1,0:T(8,128)} %bitcast.19, f32[]{:T(128)} %constant.13.clone.1), dimensions={0}, to_apply=%region_2.3 | reduce | flops 7864320 | bytes 35651588 | tf_op jit(solution)/shard_map/reduce_sum | solution.py:11
  729.7 3.5 fusion.49
  733.3 1.0 copy-done.10
  734.3 3.9 fusion.28
  738.2 0.0 reduce-scatter.2.cloned.1.call-update
  738.2 0.7 copy-done.17
  738.9 1.8 gather_fusion.2
  740.7 1.4 multiply_reduce_fusion
  742.1 3.7 scatter_custom_fusion
  745.8 0.0 copy-done.1
  745.8 4.1 convolution_add_fusion
  749.9 0.0 copy-start.2
  749.9 0.0 copy-start.4
  749.9 0.1 multiply_add_fusion.7
  750.0 0.1 multiply_add_fusion.9
  750.1 0.6 copy-done.2
  750.7 2.4 scatter_custom_fusion.1
  753.1 1.2 add_any.115
  754.3 4.8 all-to-all-start.1
  759.1 0.0 all-reduce.3.cloned.1.call-start
  759.2 0.1 multiply_add_fusion.5
  759.2 0.1 multiply_add_fusion.4
  759.3 0.0 copy-done.6
  759.3 0.0 copy-done.14
  759.4 0.0 copy-done.20
  759.4 0.0 copy-start.11
  759.4 0.0 copy-start.12
  759.4 0.4 multiply_negate_fusion
  759.8 0.1 add_multiply_fusion.3
  759.9 0.7 maximum_add_fusion
  760.6 125.8 %reduce-scatter.2.cloned.1.call-done = f32[32,512]{1,0:T(8,128)} async-done(((f32[1024,512]{1,0:T(8,128)}), f32[32,512]{1,0:T(8,128)}) %reduce-scatter.2.cloned.1.call-update) | async-done | bytes 65552 | tf_op jit(solution)/shard_map/reduce_scatter | solution.py:90
  886.4 0.0 all-reduce.3.cloned.1.call-update
  886.4 0.0 all-to-all-done.1
  886.4 3.6 scatter_custom_fusion.2
  890.1 188.2 %all-reduce.3.cloned.1.call-done = (f32[32,512]{1,0:T(8,128)}, f32[128,512]{1,0:T(8,128)}) async-done(((f32[32,512]{1,0:T(8,128)}, f32[128,512]{1,0:T(8,128)}), (f32[32,512]{1,0:T(8,128)}, f32[128,512]{1,0:T(8,128)})) %all-reduce.3.cloned.1.call-update) | async-done | bytes 327696 | tf_op jit(solution)/shard_map/psum | solution.py:91
  1078.2 1.2 scatter_custom_fusion.3
  1079.5 2.0 multiply_subtract_fusion
  (33 shorter events, 0.2 us)
Async XLA Ops:
  7.2 71.0 %all-gather.5.cloned.1.call-start = ((), (), s32[]{:S(2)}) async-start(), calls=%async_computation.4 | async-start | bytes 2162688 | tf_op jit(solution)/shard_map/all_gather | solution.py:74
  7.9 0.5 copy-start.18
  10.7 705.0 %all-gather.7.cloned.1.call-start = ((), (), s32[]{:S(2)}) async-start(), calls=%async_computation.5 | async-start | bytes 35651584 | tf_op jit(solution)/shard_map/all_gather | solution.py:10
  79.7 0.7 copy-start.15
  79.7 1.0 copy-start
  83.0 5.5 copy-start.16
  83.0 5.5 copy-start.5
  83.0 5.6 copy-start.19
  83.0 76.6 %all-to-all-start = ((f32[32,16,512]{2,1,0:T(8,128)}), f32[32,16,512]{2,1,0:T(8,128)S(1)}, u32[]{:S(2)}, u32[]{:S(2)}) async-start(f32[32,16,512]{2,1,0:T(8,128)} %bitcast.1), calls=%async_computation | async-start | bytes 2097152 | tf_op jit(solution)/shard_map/all_to_all | solution.py:68
  88.4 798.0 %reduce-scatter.2.cloned.1.call-start = ((), (), s32[]{:S(2)}) async-start(), calls=%async_computation.3 | async-start | bytes 2162688 | tf_op jit(solution)/shard_map/reduce_scatter | solution.py:90
  88.6 71.0 %copy-start.13 = (f32[128,128]{1,0:T(8,128)}, f32[128,128]{1,0:T(8,128)S(1)}, u32[]{:S(2)}) copy-start(f32[128,128]{1,0:T(8,128)S(1)} %add_sqrt_fusion) | copy-start | bytes 196612
  160.6 572.6 %copy-start.7 = (f32[256,128]{1,0:T(8,128)}, f32[256,128]{1,0:T(8,128)S(1)}, u32[]{:S(2)}) copy-start(f32[256,128]{1,0:T(8,128)S(1)} %get-tuple-element.23) | copy-start | bytes 393220
  160.7 572.5 %copy-start.8 = (f32[256,128]{1,0:T(8,128)}, f32[256,128]{1,0:T(8,128)S(1)}, u32[]{:S(2)}) copy-start(f32[256,128]{1,0:T(8,128)S(1)} %get-tuple-element.20) | copy-start | bytes 393220
  160.7 572.5 %copy-start.9 = (f32[256,128]{1,0:T(8,128)}, f32[256,128]{1,0:T(8,128)S(1)}, u32[]{:S(2)}) copy-start(f32[256,128]{1,0:T(8,128)S(1)} %get-tuple-element.21) | copy-start | bytes 393220
  733.3 1.0 copy-start.10
  738.2 0.7 copy-start.17
  740.7 5.1 copy-start.1
  749.9 0.8 copy-start.2
  749.9 3.2 copy-start.4
  753.1 6.1 copy-start.3
  754.3 5.0 copy-start.6
  754.3 5.0 copy-start.14
  754.3 5.0 copy-start.20
  754.3 132.1 %all-to-all-start.1 = ((f32[32,16,512]{2,1,0:T(8,128)}), f32[32,16,512]{2,1,0:T(8,128)S(1)}, u32[]{:S(2)}, u32[]{:S(2)}) async-start(f32[32,16,512]{2,1,0:T(8,128)} %bitcast.7), calls=%async_computation.1 | async-start | bytes 2097152 | tf_op jit(solution)/shard_map/all_to_all | solution.py:82
  759.1 319.1 %all-reduce.3.cloned.1.call-start = ((), (), s32[]{:S(2)}) async-start(), calls=%async_computation.6 | async-start | bytes 655360 | tf_op jit(solution)/shard_map/psum | solution.py:91
  759.4 320.1 %copy-start.11 = (f32[128,512]{1,0:T(8,128)S(1)}, f32[128,512]{1,0:T(8,128)}, u32[]{:S(2)}) copy-start(f32[128,512]{1,0:T(8,128)} %param.13) | copy-start | bytes 786436
  759.4 320.1 %copy-start.12 = (f32[128,512]{1,0:T(8,128)S(1)}, f32[128,512]{1,0:T(8,128)}, u32[]{:S(2)}) copy-start(f32[128,512]{1,0:T(8,128)} %param.11) | copy-start | bytes 786436
Sparse Core Ops, SparseCore 0:
  10.8 67.3 all-gather.4
  81.4 634.3 all-gather.6
  738.4 147.9 reduce-scatter.1
  889.8 188.3 all-reduce.2
